TPU v7x, 32 devices: a whole 2x2x4 slice. The times are simulated.
32 devices in a mesh: pair: 16 (over z, y, x), dp: 2 (over core).
Axes of the slice: x: 2, y: 2, z: 4, core: 2. Of those that a mesh axis runs over, the one named last changes fastest.
Arguments:
- features: bfloat16 [16384, 2048], P(('pair', 'dp')), may hold values from -6 to 6
- proj_weight: bfloat16 [2048, 128], replicated, may hold values from -0.01171875 to 0.01171875
- row_lse: bfloat16 [16384], P(('pair', 'dp')), may hold values from 6 to 9
- positive: int32 [16384], P(('pair', 'dp')), may hold values from 0 to 16383, as said below
Outputs:
- grad_embed: float32 [16384, 128], P(('pair', 'dp'))
- grad_weight: float32 [2048, 128], P('dp')
Inputs may be any that keep to these rules, and one draw needn't show every extreme that they name: positive[i] names the row that holds the other view of row i's cutout: positive[positive[i]] = i and positive[i] != i.
All inputs are finite; a program needn't handle non-finite values.
Results may differ from a plain program's by a relative error of at most 0.0045.
Values may be sent and summed in bfloat16 or wider, within the bound.
No kernel may reach another device: no remote copies, remote signals or barrier semaphores. Data moves between devices by JAX's collectives and lax.ppermute only.
A program may use at most 64 MiB of HBM per device.

v0:
```python
import jax
import jax.numpy as jnp
from jax import lax
from jax.sharding import PartitionSpec as P

contrastive_divisor = 0.1
epsilon = 1e-06


def from_behind(value, axis, steps):
    count = lax.axis_size(axis)
    pairs = [(source, (source + steps) % count) for source in range(count)]
    return lax.ppermute(value, axis, pairs)


def coupling_tile(embedded, own_lse, own_positive, counterpart_feature_vectors, part_lse, first_id):
    cosine_affinity_matrix = (
        lax.dot_general(
            embedded,
            counterpart_feature_vectors,
            (((1,), (1,)), ((), ())),
            preferred_element_type=jnp.float32,
        )
        / contrastive_divisor
    )
    weights = jnp.exp(cosine_affinity_matrix - own_lse.astype(jnp.float32)[:, None]) + jnp.exp(
        cosine_affinity_matrix - part_lse.astype(jnp.float32)[None, :]
    )
    identity_rows = first_id + jnp.arange(counterpart_feature_vectors.shape[0], dtype=jnp.int32)
    matched = (own_positive[:, None] == identity_rows[None, :]).astype(jnp.float32)
    return (weights - 2.0 * matched).astype(jnp.bfloat16)


def body(features, proj_weight, row_lse, positive):
    row_count = features.shape[0]
    dp_count = lax.axis_size("dp")
    pair_count = lax.axis_size("pair")
    group_rows = row_count * dp_count
    far_offset = pair_count // 4
    my_block = lax.axis_index("pair")
    projected = jnp.dot(features, proj_weight, preferred_element_type=jnp.float32)
    magnitude = jnp.sqrt(jnp.sum(projected * projected, axis=-1, keepdims=True) + epsilon)
    unit_vectors = projected / magnitude
    embedded = unit_vectors.astype(jnp.bfloat16)
    whole_embed, whole_lse = (
        lax.all_gather(embedded, "dp", axis=0, tiled=True),
        lax.all_gather(row_lse, "dp", axis=0, tiled=True),
    )
    upstream_derivative = jnp.zeros((row_count, embedded.shape[1]), jnp.float32)
    for offset in (1, far_offset):
        counterpart_feature_vectors, part_lse = from_behind(
            (whole_embed, whole_lse), "pair", offset
        )
        part_block = jnp.remainder(my_block - offset, pair_count)
        tile_coupling = coupling_tile(
            embedded,
            row_lse,
            positive,
            counterpart_feature_vectors,
            part_lse,
            part_block * group_rows,
        )
        coupling, counterpart_feature_vectors = (tile_coupling, counterpart_feature_vectors)
        upstream_derivative = upstream_derivative + jnp.dot(
            coupling, counterpart_feature_vectors, preferred_element_type=jnp.float32
        )
        returned = lax.psum_scatter(
            lax.dot_general(
                coupling, embedded, (((0,), (0,)), ((), ())), preferred_element_type=jnp.float32
            ),
            "dp",
            scatter_dimension=0,
            tiled=True,
        )
        upstream_derivative = upstream_derivative + from_behind(returned, "pair", -offset)
    derivative_pair_affinity = upstream_derivative / contrastive_divisor
    grad_embed = (
        derivative_pair_affinity
        - unit_vectors * jnp.sum(unit_vectors * derivative_pair_affinity, axis=-1, keepdims=True)
    ) / magnitude
    grad_half = grad_embed.astype(jnp.bfloat16)
    local_term = lax.dot_general(
        features, grad_half, (((0,), (0,)), ((), ())), preferred_element_type=jnp.float32
    )
    summed = lax.psum(local_term, "pair")
    grad_weight = lax.psum_scatter(summed, "dp", scatter_dimension=0, tiled=True)
    return (grad_embed, grad_weight)


def solution(mesh):
    return jax.shard_map(
        body,
        mesh=mesh,
        in_specs=(P(("pair", "dp"), None), P(), P(("pair", "dp")), P(("pair", "dp"))),
        out_specs=(P(("pair", "dp"), None), P("dp", None)),
        check_vma=False,
    )
```

profile of v0, /device:TPU:0, one launch (start us, length us, event | category | flops | bytes accessed | tf_op | source)
XLA Modules:
  0.0 204.0 jit_solution(16239086399272684663)
XLA Ops:
  7.2 1.5 copy-done
  8.8 1.9 multiply_reduce_fusion.1
  10.7 2.1 %all_gather.6 = bf16[1024,128]{0,1:T(8,128)(2,1)S(1)} all-gather(bf16[512,128]{0,1:T(8,128)(2,1)S(1)} %fusion.4), channel_id=1, replica_groups=mesh['pair'=16,'dp'=2] {'dp'}, dimensions={0}, use_global_device_ids=true | all-gather | bytes 393216 | tf_op jit(solution)/shard_map/all_gather | solution.py:46
  12.8 2.9 %collective-permute-start.3 = (bf16[1024,128]{0,1:T(8,128)(2,1)S(1)}, bf16[1024,128]{0,1:T(8,128)(2,1)S(1)}, u32[]{:S(2)}, u32[]{:S(2)}) collective-permute-start(bf16[1024,128]{0,1:T(8,128)(2,1)S(1)} %all_gather.6), channel_id=1, source_target_pairs={{0,8},{2,10},{4,12},{6,14},{8,16},{10,18},{12,20},{14,22},{16,24},... | collective-permute-start | bytes 786440 | tf_op jit(solution)/shard_map/ppermute | solution.py:13
  15.7 1.8 all-gather
  17.5 1.6 collective-permute-start.4
  19.2 1.5 collective-permute-start.1
  20.7 1.5 collective-permute-start
  22.1 2.3 %collective-permute-done.4 = bf16[1024]{0:T(1024)(128)(2,1)S(1)} collective-permute-done((bf16[1024]{0:T(1024)(128)(2,1)S(1)}, bf16[1024]{0:T(1024)(128)(2,1)S(1)}, u32[]{:S(2)}, u32[]{:S(2)}) %collective-permute-start.4) | collective-permute-done | bytes 2080 | tf_op jit(solution)/shard_map/ppermute | solution.py:13
  24.4 1.9 collective-permute-done.1
  26.8 5.3 %collective-permute-done = bf16[1024,128]{0,1:T(8,128)(2,1)S(1)} collective-permute-done((bf16[1024,128]{0,1:T(8,128)(2,1)S(1)}, bf16[1024,128]{0,1:T(8,128)(2,1)S(1)}, u32[]{:S(2)}, u32[]{:S(2)}) %collective-permute-start) | collective-permute-done | bytes 262176 | tf_op jit(solution)/shard_map/ppermute | solution.py:13
  32.8 3.0 %subtract_convert_fusion.1 = (bf16[512,1024]{1,0:T(8,128)(2,1)S(1)}, bf16[512,1024]{1,0:T(8,128)(2,1)S(1)}) fusion(s32[1024]{0:T(1024)S(1)} %get-tuple-element.15, f32[1024]{0:T(1024)S(1)} %convert_element_type.26, f32[512]{0:T(512)S(1)} %convert_element_type.25, s32[512]{0:T(512)S(1)} %copy-done.5, s32[1024]{0:T(1024)S(1)} %get-tuple-element.14, ...), kind=kOutput, calls=%fused_computation.2 | convolution fusion | flops 142606336 | bytes 4608000 | tf_op jit(solution)/shard_map/dot_general | solution.py:18
  37.9 1.1 fusion.7
  39.1 4.2 %reduce-scatter.6.cloned.1.call-done = f32[512,128]{0,1:T(8,128)} async-done(((f32[1024,128]{0,1:T(8,128)}), f32[512,128]{0,1:T(8,128)}) %reduce-scatter.6.cloned.1.call-update) | async-done | bytes 262160 | tf_op jit(solution)/shard_map/reduce_scatter | solution.py:67
  43.4 3.6 %collective-permute-start.5 = (f32[512,128]{0,1:T(8,128)}, f32[512,128]{0,1:T(8,128)}, u32[]{:S(2)}, u32[]{:S(2)}) collective-permute-start(f32[512,128]{0,1:T(8,128)} %reduce-scatter.6.cloned.1.call-done), channel_id=1, source_target_pairs={{0,24},{2,26},{4,28},{6,30},{8,0},{10,2},{12,4},{14,6},{16,8},{18,... | collective-permute-start | bytes 786440 | tf_op jit(solution)/shard_map/ppermute | solution.py:13
  46.9 7.9 %reduce-scatter.4.cloned.1.call-done = f32[512,128]{0,1:T(8,128)} async-done(((f32[1024,128]{0,1:T(8,128)}), f32[512,128]{0,1:T(8,128)}) %reduce-scatter.4.cloned.1.call-update) | async-done | bytes 262160 | tf_op jit(solution)/shard_map/reduce_scatter | solution.py:67
  54.8 5.4 %collective-permute-start.2 = (f32[512,128]{0,1:T(8,128)}, f32[512,128]{0,1:T(8,128)S(1)}, u32[]{:S(2)}, u32[]{:S(2)}) collective-permute-start(f32[512,128]{0,1:T(8,128)} %reduce-scatter.4.cloned.1.call-done), channel_id=1, source_target_pairs={{0,30},{2,0},{4,2},{6,4},{8,6},{10,8},{12,10},{14,12},{16,14},{18,... | collective-permute-start | bytes 786440 | tf_op jit(solution)/shard_map/ppermute | solution.py:13
  60.2 1.7 fusion.6
  62.0 4.6 %collective-permute-done.2 = f32[512,128]{0,1:T(8,128)S(1)} collective-permute-done((f32[512,128]{0,1:T(8,128)}, f32[512,128]{0,1:T(8,128)S(1)}, u32[]{:S(2)}, u32[]{:S(2)}) %collective-permute-start.2) | collective-permute-done | bytes 262176 | tf_op jit(solution)/shard_map/ppermute | solution.py:13
  66.6 1.6 multiply_reduce_fusion
  68.2 1.4 convolution_bitcast_fusion
  69.7 10.4 %reduce-scatter.8.cloned.1.call-done = f32[1024,128]{0,1:T(8,128)} async-done(((f32[2048,128]{0,1:T(8,128)}), f32[1024,128]{0,1:T(8,128)}) %reduce-scatter.8.cloned.1.call-update) | async-done | bytes 524304 | tf_op jit(solution)/shard_map/reduce_scatter | solution.py:86
  80.9 114.5 %all-reduce.2.cloned.1.call-done = f32[1024,128]{0,1:T(8,128)} async-done(((f32[1024,128]{0,1:T(8,128)}), f32[1024,128]{0,1:T(8,128)}) %all-reduce.2.cloned.1.call-update) | async-done | bytes 524304 | tf_op jit(solution)/shard_map/psum | solution.py:85
  195.4 2.0 copy.17
  (34 shorter events, 4.4 us)
Async XLA Ops:
  7.2 1.6 copy-start
  7.2 8.5 %copy-start.4 = (bf16[512]{0:T(512)(128)(2,1)S(1)}, bf16[512]{0:T(512)(128)(2,1)}, u32[]{:S(2)}) copy-start(bf16[512]{0:T(512)(128)(2,1)} %param.6) | copy-start | bytes 3076
  7.2 36.2 %reduce-scatter.6.cloned.1.call-start = ((), (), s32[]{:S(2)}) async-start(), calls=%async_computation.4 | async-start | bytes 786432 | tf_op jit(solution)/shard_map/reduce_scatter | solution.py:67
  10.6 22.2 %copy-start.5 = (s32[512]{0:T(512)S(1)}, s32[512]{0:T(512)}, u32[]{:S(2)}) copy-start(s32[512]{0:T(512)} %param.7) | copy-start | bytes 6148
  12.8 13.6 %collective-permute-start.3 = (bf16[1024,128]{0,1:T(8,128)(2,1)S(1)}, bf16[1024,128]{0,1:T(8,128)(2,1)S(1)}, u32[]{:S(2)}, u32[]{:S(2)}) collective-permute-start(bf16[1024,128]{0,1:T(8,128)(2,1)S(1)} %all_gather.6), channel_id=1, source_target_pairs={{0,8},{2,10},{4,12},{6,14},{8,16},{10,18},{12,20},{14,22},{16,24},... | collective-permute-start | bytes 786440 | tf_op jit(solution)/shard_map/ppermute | solution.py:13
  17.5 6.9 %collective-permute-start.4 = (bf16[1024]{0:T(1024)(128)(2,1)S(1)}, bf16[1024]{0:T(1024)(128)(2,1)S(1)}, u32[]{:S(2)}, u32[]{:S(2)}) collective-permute-start(bf16[1024]{0:T(1024)(128)(2,1)S(1)} %bitcast.20), channel_id=1, source_target_pairs={{0,8},{2,10},{4,12},{6,14},{8,16},{10,18},{12,20},{14,22},{16,24},... | collective-permute-start | bytes 6152 | tf_op jit(solution)/shard_map/ppermute | solution.py:13
  19.2 7.2 %collective-permute-start.1 = (bf16[1024]{0:T(1024)(128)(2,1)S(1)}, bf16[1024]{0:T(1024)(128)(2,1)S(1)}, u32[]{:S(2)}, u32[]{:S(2)}) collective-permute-start(bf16[1024]{0:T(1024)(128)(2,1)S(1)} %bitcast.21), channel_id=1, source_target_pairs={{0,2},{2,4},{4,6},{6,8},{8,10},{10,12},{12,14},{14,16},{16,18},{18... | collective-permute-start | bytes 6152 | tf_op jit(solution)/shard_map/ppermute | solution.py:13
  20.7 11.5 %collective-permute-start = (bf16[1024,128]{0,1:T(8,128)(2,1)S(1)}, bf16[1024,128]{0,1:T(8,128)(2,1)S(1)}, u32[]{:S(2)}, u32[]{:S(2)}) collective-permute-start(bf16[1024,128]{0,1:T(8,128)(2,1)S(1)} %all_gather.6), channel_id=1, source_target_pairs={{0,2},{2,4},{4,6},{6,8},{8,10},{10,12},{12,14},{14,16},{16,18},{18... | collective-permute-start | bytes 786440 | tf_op jit(solution)/shard_map/ppermute | solution.py:13
  26.3 5.8 %copy-start.2 = (bf16[1024,128]{0,1:T(8,128)(2,1)}, bf16[1024,128]{0,1:T(8,128)(2,1)S(1)}, u32[]{:S(2)}) copy-start(bf16[1024,128]{0,1:T(8,128)(2,1)S(1)} %collective-permute-done.3) | copy-start | bytes 786436
  32.1 0.7 copy-start.3
  35.8 1.0 copy-start.1
  37.9 17.0 %reduce-scatter.4.cloned.1.call-start = ((), (), s32[]{:S(2)}) async-start(), calls=%async_computation.3 | async-start | bytes 786432 | tf_op jit(solution)/shard_map/reduce_scatter | solution.py:67
  39.1 41.0 %reduce-scatter.8.cloned.1.call-start = ((), (), s32[]{:S(2)}) async-start(), calls=%async_computation.5 | async-start | bytes 1572864 | tf_op jit(solution)/shard_map/reduce_scatter | solution.py:86
  43.4 18.6 %collective-permute-start.5 = (f32[512,128]{0,1:T(8,128)}, f32[512,128]{0,1:T(8,128)}, u32[]{:S(2)}, u32[]{:S(2)}) collective-permute-start(f32[512,128]{0,1:T(8,128)} %reduce-scatter.6.cloned.1.call-done), channel_id=1, source_target_pairs={{0,24},{2,26},{4,28},{6,30},{8,0},{10,2},{12,4},{14,6},{16,8},{18,... | collective-permute-start | bytes 786440 | tf_op jit(solution)/shard_map/ppermute | solution.py:13
  54.8 11.7 %collective-permute-start.2 = (f32[512,128]{0,1:T(8,128)}, f32[512,128]{0,1:T(8,128)S(1)}, u32[]{:S(2)}, u32[]{:S(2)}) collective-permute-start(f32[512,128]{0,1:T(8,128)} %reduce-scatter.4.cloned.1.call-done), channel_id=1, source_target_pairs={{0,30},{2,0},{4,2},{6,4},{8,6},{10,8},{12,10},{14,12},{16,14},{18,... | collective-permute-start | bytes 786440 | tf_op jit(solution)/shard_map/ppermute | solution.py:13
  69.6 125.8 %all-reduce.2.cloned.1.call-start = ((), (), s32[]{:S(2)}) async-start(), calls=%async_computation.6 | async-start | bytes 1048576 | tf_op jit(solution)/shard_map/psum | solution.py:85
Sparse Core Ops, SparseCore 0:
  38.0 5.3 reduce-scatter.5
  45.7 9.1 reduce-scatter.3
  69.8 10.2 reduce-scatter.7
  85.9 109.4 all-reduce.1
where the time goes:
time: 204 us
  waiting for transfers between devices  151 us (74%)
  starting transfers between devices  16.6 us (8%)
  between operations  13.9 us (7%)
  matrix products  12.2 us (6%)
  local copies, waits for them, and re-layouts  6.09 us (3%)
  blocking collectives  3.86 us (2%)
    psum x1, waiting for transfers between devices, body(): summed = lax.psum(local_term, 'pair')  114 us
    ppermute x6, starting transfers between devices, from_behind(): return lax.ppermute(value, axis, pairs)  16.5 us
    ppermute x6, waiting for transfers between devices, from_behind(): return lax.ppermute(value, axis, pairs)  14.1 us
    reduce_scatter x2, waiting for transfers between devices, body(): lax.psum_scatter(lax.dot_general(coupling, embedded, (((0,), (0,)), ((),...  12.2 us
    reduce_scatter x1, waiting for transfers between devices, body(): lax.psum_scatter(summed, 'dp', scatter_dimension=0, tiled=True)  10.4 us
    unnamed x16, local copies, waits for them, and re-layouts  6.09 us
  transfers between devices with their start and end apart: 10, of which 8 were waited for; matrix products, arithmetic and copies ran while one was open for 2% of the time, Pallas kernels for 0%

commit v1 on v0

--- a/solution.py
+++ b/solution.py
@@ -5,6 +5,17 @@
 
 contrastive_divisor = 0.1
 epsilon = 1e-06
+
+
+def divide_the_views(my_data):
+    size_here = jax.lax.axis_size("pair")
+    tile_out = my_data
+    for c in [
+        [(pp, pp ^ nth) for pp in range(size_here)] for nth in (1, 2, 4, 8, 16) if nth < size_here
+    ]:
+        next_value = jax.lax.ppermute(tile_out, axis_name="pair", perm=c)
+        tile_out = tile_out + next_value
+    return tile_out
 
 
 def from_behind(value, axis, steps):
@@ -82,7 +93,7 @@
     local_term = lax.dot_general(
         features, grad_half, (((0,), (0,)), ((), ())), preferred_element_type=jnp.float32
     )
-    summed = lax.psum(local_term, "pair")
+    summed = divide_the_views(local_term)
     grad_weight = lax.psum_scatter(summed, "dp", scatter_dimension=0, tiled=True)
     return (grad_embed, grad_weight)
 

time: 204 us -> 206 us (level)
  starting transfers between devices: 16.6 us -> 20.6 us
  waiting for transfers between devices: 151 us -> 148 us
    psum x1 -> x0, waiting for transfers between devices: 114 us -> none  [body(): summed = lax.psum(local_term, 'pair')]
    ppermute x0 -> x4, waiting for transfers between devices: none -> 114 us  [divide_the_views(): next_value = jax.lax.ppermute(tile_out, axis_name='pair', perm=c)]
    ppermute x0 -> x4, starting transfers between devices: none -> 4.03 us  [divide_the_views(): next_value = jax.lax.ppermute(tile_out, axis_name='pair', perm=c)]
    reduce_scatter x1, waiting for transfers between devices: 10.4 us -> 7.99 us  [body(): lax.psum_scatter(summed, 'dp', scatter_dimension=0, tiled=True)]
  transfers between devices with their start and end apart: 10 -> 13, of which waited for: 8 -> 11; matrix products, arithmetic and copies ran while one was open for 2% -> 2% of each run, Pallas kernels for 0% -> 0%
where the time goes in v1:
time: 206 us
  waiting for transfers between devices  148 us (72%)
  starting transfers between devices  20.6 us (10%)
  between operations  13.9 us (7%)
  matrix products  11.3 us (5%)
  local copies, waits for them, and re-layouts  6.09 us (3%)
  blocking collectives  3.86 us (2%)
    ppermute x4, waiting for transfers between devices, divide_the_views(): next_value = jax.lax.ppermute(tile_out, axis_name='pair', perm=c)  114 us
    ppermute x6, starting transfers between devices, from_behind(): return lax.ppermute(value, axis, pairs)  16.5 us
    ppermute x6, waiting for transfers between devices, from_behind(): return lax.ppermute(value, axis, pairs)  14.1 us
    reduce_scatter x2, waiting for transfers between devices, body(): lax.psum_scatter(lax.dot_general(coupling, embedded, (((0,), (0,)), ((),...  12.1 us
    reduce_scatter x1, waiting for transfers between devices, body(): lax.psum_scatter(summed, 'dp', scatter_dimension=0, tiled=True)  7.99 us
    unnamed x16, local copies, waits for them, and re-layouts  6.09 us
  transfers between devices with their start and end apart: 13, of which 11 were waited for; matrix products, arithmetic and copies ran while one was open for 2% of the time, Pallas kernels for 0%

profile of v1, /device:TPU:0, one launch (start us, length us, event | category | flops | bytes accessed | tf_op | source)
XLA Modules:
  0.0 205.7 jit_solution(5898423274914004291)
XLA Ops:
  7.2 1.5 copy-done
  8.8 1.9 multiply_reduce_fusion.1
  10.7 2.1 %all_gather.6 = bf16[1024,128]{0,1:T(8,128)(2,1)S(1)} all-gather(bf16[512,128]{0,1:T(8,128)(2,1)S(1)} %fusion.4), channel_id=1, replica_groups=mesh['pair'=16,'dp'=2] {'dp'}, dimensions={0}, use_global_device_ids=true | all-gather | bytes 393216 | tf_op jit(solution)/shard_map/all_gather | solution.py:57
  12.8 2.9 %collective-permute-start.3 = (bf16[1024,128]{0,1:T(8,128)(2,1)S(1)}, bf16[1024,128]{0,1:T(8,128)(2,1)S(1)}, u32[]{:S(2)}, u32[]{:S(2)}) collective-permute-start(bf16[1024,128]{0,1:T(8,128)(2,1)S(1)} %all_gather.6), channel_id=1, source_target_pairs={{0,8},{2,10},{4,12},{6,14},{8,16},{10,18},{12,20},{14,22},{16,24},... | collective-permute-start | bytes 786440 | tf_op jit(solution)/shard_map/ppermute | solution.py:24
  15.7 1.8 all-gather
  17.5 1.6 collective-permute-start.4
  22.1 2.3 %collective-permute-done.4 = bf16[1024]{0:T(1024)(128)(2,1)S(1)} collective-permute-done((bf16[1024]{0:T(1024)(128)(2,1)S(1)}, bf16[1024]{0:T(1024)(128)(2,1)S(1)}, u32[]{:S(2)}, u32[]{:S(2)}) %collective-permute-start.4) | collective-permute-done | bytes 2080 | tf_op jit(solution)/shard_map/ppermute | solution.py:24
  24.4 1.9 collective-permute-done.1
  26.8 5.3 %collective-permute-done = bf16[1024,128]{0,1:T(8,128)(2,1)S(1)} collective-permute-done((bf16[1024,128]{0,1:T(8,128)(2,1)S(1)}, bf16[1024,128]{0,1:T(8,128)(2,1)S(1)}, u32[]{:S(2)}, u32[]{:S(2)}) %collective-permute-start) | collective-permute-done | bytes 262176 | tf_op jit(solution)/shard_map/ppermute | solution.py:24
  32.8 3.0 %subtract_convert_fusion.1 = (bf16[512,1024]{1,0:T(8,128)(2,1)S(1)}, bf16[512,1024]{1,0:T(8,128)(2,1)S(1)}) fusion(s32[1024]{0:T(1024)S(1)} %get-tuple-element.15, f32[1024]{0:T(1024)S(1)} %convert_element_type.26, f32[512]{0:T(512)S(1)} %convert_element_type.25, s32[512]{0:T(512)S(1)} %copy-done.5, s32[1024]{0:T(1024)S(1)} %get-tuple-element.14, ...), kind=kOutput, calls=%fused_computation.2 | convolution fusion | flops 142606336 | bytes 4608000 | tf_op jit(solution)/shard_map/dot_general | solution.py:29
  39.1 4.2 %reduce-scatter.6.cloned.1.call-done = f32[512,128]{0,1:T(8,128)} async-done(((f32[1024,128]{0,1:T(8,128)}), f32[512,128]{0,1:T(8,128)}) %reduce-scatter.6.cloned.1.call-update) | async-done | bytes 262160 | tf_op jit(solution)/shard_map/reduce_scatter | solution.py:78
  43.4 3.5 %collective-permute-start.5 = (f32[512,128]{0,1:T(8,128)}, f32[512,128]{0,1:T(8,128)}, u32[]{:S(2)}, u32[]{:S(2)}) collective-permute-start(f32[512,128]{0,1:T(8,128)} %reduce-scatter.6.cloned.1.call-done), channel_id=1, source_target_pairs={{0,24},{2,26},{4,28},{6,30},{8,0},{10,2},{12,4},{14,6},{16,8},{18,... | collective-permute-start | bytes 786440 | tf_op jit(solution)/shard_map/ppermute | solution.py:24
  46.9 7.9 %reduce-scatter.4.cloned.1.call-done = f32[512,128]{0,1:T(8,128)} async-done(((f32[1024,128]{0,1:T(8,128)}), f32[512,128]{0,1:T(8,128)}) %reduce-scatter.4.cloned.1.call-update) | async-done | bytes 262160 | tf_op jit(solution)/shard_map/reduce_scatter | solution.py:78
  54.8 5.4 %collective-permute-start.2 = (f32[512,128]{0,1:T(8,128)}, f32[512,128]{0,1:T(8,128)S(1)}, u32[]{:S(2)}, u32[]{:S(2)}) collective-permute-start(f32[512,128]{0,1:T(8,128)} %reduce-scatter.4.cloned.1.call-done), channel_id=1, source_target_pairs={{0,30},{2,0},{4,2},{6,4},{8,6},{10,8},{12,10},{14,12},{16,14},{18,... | collective-permute-start | bytes 786440 | tf_op jit(solution)/shard_map/ppermute | solution.py:24
  60.2 1.7 fusion.6
  62.0 4.6 %collective-permute-done.2 = f32[512,128]{0,1:T(8,128)S(1)} collective-permute-done((f32[512,128]{0,1:T(8,128)}, f32[512,128]{0,1:T(8,128)S(1)}, u32[]{:S(2)}, u32[]{:S(2)}) %collective-permute-start.2) | collective-permute-done | bytes 262176 | tf_op jit(solution)/shard_map/ppermute | solution.py:24
  66.6 1.6 multiply_reduce_fusion
  68.7 24.6 %collective-permute-done.6 = f32[2048,128]{0,1:T(8,128)S(1)} collective-permute-done((f32[2048,128]{0,1:T(8,128)S(1)}, f32[2048,128]{0,1:T(8,128)S(1)}, u32[]{:S(2)}, u32[]{:S(2)}) %collective-permute-start.6) | collective-permute-done | bytes 1048608 | tf_op jit(solution)/shard_map/ppermute | solution.py:16
  93.7 23.5 %collective-permute-done.7 = f32[2048,128]{0,1:T(8,128)S(1)} collective-permute-done((f32[2048,128]{0,1:T(8,128)S(1)}, f32[2048,128]{0,1:T(8,128)S(1)}, u32[]{:S(2)}, u32[]{:S(2)}) %collective-permute-start.7) | collective-permute-done | bytes 1048608 | tf_op jit(solution)/shard_map/ppermute | solution.py:16
  117.6 22.5 %collective-permute-done.8 = f32[2048,128]{0,1:T(8,128)S(1)} collective-permute-done((f32[2048,128]{0,1:T(8,128)S(1)}, f32[2048,128]{0,1:T(8,128)S(1)}, u32[]{:S(2)}, u32[]{:S(2)}) %collective-permute-start.8) | collective-permute-done | bytes 1048608 | tf_op jit(solution)/shard_map/ppermute | solution.py:16
  140.3 3.4 %collective-permute-start.9 = (f32[2048,128]{0,1:T(8,128)S(1)}, f32[2048,128]{0,1:T(8,128)S(1)}, u32[]{:S(2)}, u32[]{:S(2)}) collective-permute-start(f32[2048,128]{0,1:T(8,128)S(1)} %add.88), channel_id=1, source_target_pairs={{0,16},{2,18},{4,20},{6,22},{8,24},{10,26},{12,28},{14,30},{16,0},... | collective-permute-start | bytes 3145736 | tf_op jit(solution)/shard_map/ppermute | solution.py:16
  143.7 43.4 %collective-permute-done.9 = f32[2048,128]{0,1:T(8,128)S(1)} collective-permute-done((f32[2048,128]{0,1:T(8,128)S(1)}, f32[2048,128]{0,1:T(8,128)S(1)}, u32[]{:S(2)}, u32[]{:S(2)}) %collective-permute-start.9) | collective-permute-done | bytes 1048608 | tf_op jit(solution)/shard_map/ppermute | solution.py:16
  189.1 8.0 %reduce-scatter.8.cloned.1.call-done = f32[1024,128]{0,1:T(8,128)} async-done(((f32[2048,128]{0,1:T(8,128)}), f32[1024,128]{0,1:T(8,128)}) %reduce-scatter.8.cloned.1.call-update) | async-done | bytes 524304 | tf_op jit(solution)/shard_map/reduce_scatter | solution.py:97
  197.1 2.0 copy.17
  (43 shorter events, 11.0 us)
Async XLA Ops:
  7.2 1.6 copy-start
  7.2 8.5 %copy-start.4 = (bf16[512]{0:T(512)(128)(2,1)S(1)}, bf16[512]{0:T(512)(128)(2,1)}, u32[]{:S(2)}) copy-start(bf16[512]{0:T(512)(128)(2,1)} %param.6) | copy-start | bytes 3076
  7.2 36.2 %reduce-scatter.6.cloned.1.call-start = ((), (), s32[]{:S(2)}) async-start(), calls=%async_computation.4 | async-start | bytes 786432 | tf_op jit(solution)/shard_map/reduce_scatter | solution.py:78
  10.6 22.2 %copy-start.5 = (s32[512]{0:T(512)S(1)}, s32[512]{0:T(512)}, u32[]{:S(2)}) copy-start(s32[512]{0:T(512)} %param.7) | copy-start | bytes 6148
  12.8 13.6 %collective-permute-start.3 = (bf16[1024,128]{0,1:T(8,128)(2,1)S(1)}, bf16[1024,128]{0,1:T(8,128)(2,1)S(1)}, u32[]{:S(2)}, u32[]{:S(2)}) collective-permute-start(bf16[1024,128]{0,1:T(8,128)(2,1)S(1)} %all_gather.6), channel_id=1, source_target_pairs={{0,8},{2,10},{4,12},{6,14},{8,16},{10,18},{12,20},{14,22},{16,24},... | collective-permute-start | bytes 786440 | tf_op jit(solution)/shard_map/ppermute | solution.py:24
  17.5 6.9 %collective-permute-start.4 = (bf16[1024]{0:T(1024)(128)(2,1)S(1)}, bf16[1024]{0:T(1024)(128)(2,1)S(1)}, u32[]{:S(2)}, u32[]{:S(2)}) collective-permute-start(bf16[1024]{0:T(1024)(128)(2,1)S(1)} %bitcast.20), channel_id=1, source_target_pairs={{0,8},{2,10},{4,12},{6,14},{8,16},{10,18},{12,20},{14,22},{16,24},... | collective-permute-start | bytes 6152 | tf_op jit(solution)/shard_map/ppermute | solution.py:24
  19.2 7.2 %collective-permute-start.1 = (bf16[1024]{0:T(1024)(128)(2,1)S(1)}, bf16[1024]{0:T(1024)(128)(2,1)S(1)}, u32[]{:S(2)}, u32[]{:S(2)}) collective-permute-start(bf16[1024]{0:T(1024)(128)(2,1)S(1)} %bitcast.21), channel_id=1, source_target_pairs={{0,2},{2,4},{4,6},{6,8},{8,10},{10,12},{12,14},{14,16},{16,18},{18... | collective-permute-start | bytes 6152 | tf_op jit(solution)/shard_map/ppermute | solution.py:24
  20.7 11.5 %collective-permute-start = (bf16[1024,128]{0,1:T(8,128)(2,1)S(1)}, bf16[1024,128]{0,1:T(8,128)(2,1)S(1)}, u32[]{:S(2)}, u32[]{:S(2)}) collective-permute-start(bf16[1024,128]{0,1:T(8,128)(2,1)S(1)} %all_gather.6), channel_id=1, source_target_pairs={{0,2},{2,4},{4,6},{6,8},{8,10},{10,12},{12,14},{14,16},{16,18},{18... | collective-permute-start | bytes 786440 | tf_op jit(solution)/shard_map/ppermute | solution.py:24
  26.3 5.8 %copy-start.2 = (bf16[1024,128]{0,1:T(8,128)(2,1)}, bf16[1024,128]{0,1:T(8,128)(2,1)S(1)}, u32[]{:S(2)}) copy-start(bf16[1024,128]{0,1:T(8,128)(2,1)S(1)} %collective-permute-done.3) | copy-start | bytes 786436
  32.1 0.7 copy-start.3
  35.8 1.0 copy-start.1
  37.9 16.9 %reduce-scatter.4.cloned.1.call-start = ((), (), s32[]{:S(2)}) async-start(), calls=%async_computation.3 | async-start | bytes 786432 | tf_op jit(solution)/shard_map/reduce_scatter | solution.py:78
  39.1 158.0 %reduce-scatter.8.cloned.1.call-start = ((), (), s32[]{:S(2)}) async-start(), calls=%async_computation.5 | async-start | bytes 1572864 | tf_op jit(solution)/shard_map/reduce_scatter | solution.py:97
  43.4 18.6 %collective-permute-start.5 = (f32[512,128]{0,1:T(8,128)}, f32[512,128]{0,1:T(8,128)}, u32[]{:S(2)}, u32[]{:S(2)}) collective-permute-start(f32[512,128]{0,1:T(8,128)} %reduce-scatter.6.cloned.1.call-done), channel_id=1, source_target_pairs={{0,24},{2,26},{4,28},{6,30},{8,0},{10,2},{12,4},{14,6},{16,8},{18,... | collective-permute-start | bytes 786440 | tf_op jit(solution)/shard_map/ppermute | solution.py:24
  54.8 11.8 %collective-permute-start.2 = (f32[512,128]{0,1:T(8,128)}, f32[512,128]{0,1:T(8,128)S(1)}, u32[]{:S(2)}, u32[]{:S(2)}) collective-permute-start(f32[512,128]{0,1:T(8,128)} %reduce-scatter.4.cloned.1.call-done), channel_id=1, source_target_pairs={{0,30},{2,0},{4,2},{6,4},{8,6},{10,8},{12,10},{14,12},{16,14},{18,... | collective-permute-start | bytes 786440 | tf_op jit(solution)/shard_map/ppermute | solution.py:24
  68.7 24.7 %collective-permute-start.6 = (f32[2048,128]{0,1:T(8,128)S(1)}, f32[2048,128]{0,1:T(8,128)S(1)}, u32[]{:S(2)}, u32[]{:S(2)}) collective-permute-start(f32[2048,128]{0,1:T(8,128)S(1)} %convolution_bitcast_fusion), channel_id=1, source_target_pairs={{0,2},{2,0},{4,6},{6,4},{8,10},{10,8},{12,14},{14,12},{16,18},{18,... | collective-permute-start | bytes 3145736 | tf_op jit(solution)/shard_map/ppermute | solution.py:16
  93.5 23.7 %collective-permute-start.7 = (f32[2048,128]{0,1:T(8,128)S(1)}, f32[2048,128]{0,1:T(8,128)S(1)}, u32[]{:S(2)}, u32[]{:S(2)}) collective-permute-start(f32[2048,128]{0,1:T(8,128)S(1)} %add.86), channel_id=1, source_target_pairs={{0,4},{2,6},{4,0},{6,2},{8,12},{10,14},{12,8},{14,10},{16,20},{18,... | collective-permute-start | bytes 3145736 | tf_op jit(solution)/shard_map/ppermute | solution.py:16
  117.3 22.8 %collective-permute-start.8 = (f32[2048,128]{0,1:T(8,128)S(1)}, f32[2048,128]{0,1:T(8,128)S(1)}, u32[]{:S(2)}, u32[]{:S(2)}) collective-permute-start(f32[2048,128]{0,1:T(8,128)S(1)} %add.87), channel_id=1, source_target_pairs={{0,8},{2,10},{4,12},{6,14},{8,0},{10,2},{12,4},{14,6},{16,24},{18,... | collective-permute-start | bytes 3145736 | tf_op jit(solution)/shard_map/ppermute | solution.py:16
  140.3 46.9 %collective-permute-start.9 = (f32[2048,128]{0,1:T(8,128)S(1)}, f32[2048,128]{0,1:T(8,128)S(1)}, u32[]{:S(2)}, u32[]{:S(2)}) collective-permute-start(f32[2048,128]{0,1:T(8,128)S(1)} %add.88), channel_id=1, source_target_pairs={{0,16},{2,18},{4,20},{6,22},{8,24},{10,26},{12,28},{14,30},{16,0},... | collective-permute-start | bytes 3145736 | tf_op jit(solution)/shard_map/ppermute | solution.py:16
Sparse Core Ops, SparseCore 0:
  38.0 5.3 reduce-scatter.5
  45.7 9.0 reduce-scatter.3
  188.4 8.6 reduce-scatter.7
